TPU v7x, 32 devices: a whole 2x2x4 slice. The times are simulated.
32 devices in a mesh: dp: 4 (over z), freq: 2 (over core), tm: 4 (over y, x).
Axes of the slice: x: 2, y: 2, z: 4, core: 2. Of those that a mesh axis runs over, the one named last changes fastest.
Arguments:
- patches: bfloat16 [1312, 32, 768], P(('freq', 'tm'), 'dp'), may hold values from -6 to 6
- col_counts: int32 [4], replicated, may hold values from 26 to 27, as said below
- norm_gain: bfloat16 [2, 768], replicated, may hold values from 0.099609375 to 1.8984375
- norm_shift: bfloat16 [2, 768], replicated, may hold values from -3 to 3
- joint_proj: bfloat16 [768, 2304], replicated, may hold values from -0.3125 to 0.3125
- proj_bias: bfloat16 [2, 768], replicated, may hold values from -3 to 3
- out_proj: bfloat16 [768, 768], replicated, may hold values from -0.875 to 0.875
- up_proj: bfloat16 [768, 3072], replicated, may hold values from -0.21875 to 0.21875
- up_bias: bfloat16 [3072], replicated, may hold values from -3 to 3
- down_proj: bfloat16 [3072, 768], replicated, may hold values from -0.109375 to 0.109375
- out_bias: bfloat16 [2, 768], replicated, may hold values from -3 to 3
- cotangent: bfloat16 [1312, 32, 768], P(('freq', 'tm'), 'dp'), may hold values from -6 to 6
Outputs:
- output: bfloat16 [1312, 32, 768], P(('freq', 'tm'), 'dp')
- grad_patches: bfloat16 [1312, 32, 768], P(('freq', 'tm'), 'dp')
- grad_norm_gain: float32 [2, 768], P(None, ('freq', 'tm'))
- grad_norm_shift: float32 [2, 768], P(None, ('freq', 'tm'))
- grad_joint_proj: float32 [768, 2304], P(('freq', 'tm'))
- grad_proj_bias: float32 [2, 768], P(None, ('freq', 'tm'))
- grad_out_proj: float32 [768, 768], P(('freq', 'tm'))
- grad_up_proj: float32 [768, 3072], P(('freq', 'tm'))
- grad_up_bias: float32 [3072], P(('freq', 'tm'))
- grad_down_proj: float32 [3072, 768], P(('freq', 'tm'))
- grad_out_bias: float32 [2, 768], P(None, ('freq', 'tm'))
Inputs may be any that keep to these rules, and one draw needn't show every extreme that they name: `col_counts`: each entry is 26 or 27, and both occur in every draw.
All inputs are finite; a program needn't handle non-finite values.
Results may differ from a plain program's by a relative error of at most 0.019.
Values may be sent and summed in bfloat16 or wider, within the bound.
No kernel may reach another device: no remote copies, remote signals or barrier semaphores. Data moves between devices by JAX's collectives and lax.ppermute only.
A program may use at most 448 MiB of HBM per device.

v0:
```python
import math
import jax
import jax.numpy as jnp
from jax import lax
from jax.sharding import PartitionSpec as P

HEADS = 12
DH = 64
FREQ_ROWS = 12
EPS = 1e-06
NEG = -1000000000.0


def live_slots(col_counts, slot_ids, freq_ids, time_ids, freq_rows, cap_cols):
    table = jnp.arange(col_counts.shape[0], dtype=jnp.int32)
    live_cols = jnp.sum(
        jnp.where(time_ids[:, None] == table[None, :], col_counts[None, :], 0), axis=1
    )
    in_grid = slot_ids < freq_rows * cap_cols
    column_live = slot_ids // freq_rows < live_cols
    extra_live = (time_ids == 0) & (freq_ids == 0)
    return jnp.where(in_grid, column_live, extra_live)


def norm_rows(values, gain, shift):
    centered = values - jnp.mean(values, axis=-1, keepdims=True)
    inverse = lax.rsqrt(jnp.mean(centered * centered, axis=-1, keepdims=True) + EPS)
    return centered * inverse * gain + shift


def gelu_exact(values):
    return jax.nn.gelu(values, approximate=False)


def matmul(left, right):
    return jnp.dot(left, right, preferred_element_type=jnp.float32)


def matmul_tn(left, right):
    return lax.dot_general(
        left, right, (((0,), (0,)), ((), ())), preferred_element_type=jnp.float32
    )


def matmul_nt(left, right):
    return lax.dot_general(
        left, right, (((1,), (1,)), ((), ())), preferred_element_type=jnp.float32
    )


def head_pair(array, offset, lane_width, head_size):
    section = lax.dynamic_slice_in_dim(array, offset, lane_width, 2)
    return section.reshape(section.shape[0], section.shape[1], 2, head_size)


def add_lanes(target, addend, offset):
    current = lax.dynamic_slice_in_dim(target, offset, addend.shape[2], 2)
    return lax.dynamic_update_slice_in_dim(target, current + addend, offset, 2)


def pair_probs(query_pair, key_pair, log_pair, mask, scale):
    scores = (
        jnp.einsum("qchd,kchd->chqk", query_pair, key_pair, preferred_element_type=jnp.float32)
        * scale
        + mask
    )
    return jnp.exp(scores - jnp.transpose(log_pair, (1, 2, 0))[..., None])


def per_device(
    patches,
    col_counts,
    norm_gain,
    norm_shift,
    joint_proj,
    proj_bias,
    out_proj,
    up_proj,
    up_bias,
    down_proj,
    out_bias,
    cotangent,
):
    slots, clips, width = patches.shape
    row_count = slots * clips
    lane_width = 2 * DH
    pair_count = HEADS // 2
    scale = 1.0 / math.sqrt(DH)
    freq_size = lax.axis_size("freq")
    time_size = lax.axis_size("tm")
    freq_rows = FREQ_ROWS // freq_size
    cap_cols = (slots - 2) // freq_rows
    key_count = slots * freq_size * time_size
    slot_ids = jnp.arange(slots, dtype=jnp.int32)
    own_live = live_slots(
        col_counts,
        slot_ids,
        jnp.full((slots,), lax.axis_index("freq"), jnp.int32),
        jnp.full((slots,), lax.axis_index("tm"), jnp.int32),
        freq_rows,
        cap_cols,
    )
    key_ids = jnp.arange(key_count, dtype=jnp.int32)
    key_group = key_ids // slots
    key_live = live_slots(
        col_counts,
        key_ids % slots,
        key_group // time_size,
        key_group % time_size,
        freq_rows,
        cap_cols,
    )
    key_mask = jnp.where(key_live, 0.0, NEG).astype(jnp.float32)
    row_live = (
        jnp.broadcast_to(own_live[:, None], (slots, clips))
        .reshape(row_count, 1)
        .astype(jnp.float32)
    )
    gain_full = norm_gain.astype(jnp.float32)
    shift_full = norm_shift.astype(jnp.float32)
    bias_full = proj_bias.astype(jnp.float32)
    outb_full = out_bias.astype(jnp.float32)
    upb_full = up_bias.astype(jnp.float32)
    inputs = patches.reshape(row_count, width).astype(jnp.float32)
    normed1, ln1_back = jax.vjp(norm_rows, inputs, gain_full[0], shift_full[0])
    normed1_low = normed1.astype(jnp.bfloat16)
    joint = matmul(normed1_low, joint_proj)
    query_low = (joint[:, :width] + bias_full[0]).astype(jnp.bfloat16)
    keys_low = joint[:, width : 2 * width].astype(jnp.bfloat16)
    memory_low = (joint[:, 2 * width :] + bias_full[1]).astype(jnp.bfloat16)
    query3 = query_low.reshape(slots, clips, width)
    key_value = jnp.concatenate([keys_low, memory_low], axis=1).reshape(slots, clips, 2 * width)
    all_memory = lax.all_gather(key_value, ("freq", "tm"), axis=0, tiled=True)

    def forward_pair(number, state):
        mixed_acc, log_acc = state
        offset = number * lane_width
        query_pair = head_pair(query3, offset, lane_width, DH)
        key_pair = head_pair(all_memory, offset, lane_width, DH)
        value_pair = head_pair(all_memory, width + offset, lane_width, DH)
        scores = (
            jnp.einsum("qchd,kchd->chqk", query_pair, key_pair, preferred_element_type=jnp.float32)
            * scale
            + key_mask
        )
        highest = jnp.max(scores, axis=-1, keepdims=True)
        exponent = jnp.exp(scores - highest)
        summed = jnp.sum(exponent, axis=-1, keepdims=True)
        attention = (exponent / summed).astype(jnp.bfloat16)
        mixed = jnp.einsum(
            "chqk,kchd->qchd", attention, value_pair, preferred_element_type=jnp.float32
        )
        log_pair = jnp.transpose((highest + jnp.log(summed))[..., 0], (2, 0, 1))
        mixed_acc = lax.dynamic_update_slice_in_dim(
            mixed_acc, mixed.reshape(slots, clips, lane_width), offset, 2
        )
        log_acc = lax.dynamic_update_slice_in_dim(log_acc, log_pair, 2 * number, 2)
        return (mixed_acc, log_acc)

    mixed_full, log_rows = lax.fori_loop(
        0,
        pair_count,
        forward_pair,
        (
            jnp.zeros((slots, clips, width), jnp.float32),
            jnp.zeros((slots, clips, HEADS), jnp.float32),
        ),
    )
    mixed_low = mixed_full.reshape(row_count, width).astype(jnp.bfloat16)
    middle = inputs + matmul(mixed_low, out_proj) + outb_full[0]
    normed2, ln2_back = jax.vjp(norm_rows, middle, gain_full[1], shift_full[1])
    normed2_low = normed2.astype(jnp.bfloat16)
    pre_act = matmul(normed2_low, up_proj) + upb_full
    activated, gelu_back = jax.vjp(gelu_exact, pre_act)
    hidden_low = activated.astype(jnp.bfloat16)
    final = middle + matmul(hidden_low, down_proj) + outb_full[1]
    output = (final * row_live).astype(jnp.bfloat16).reshape(slots, clips, width)
    grad_out_rows = cotangent.reshape(row_count, width).astype(jnp.float32) * row_live
    grad_out_low = grad_out_rows.astype(jnp.bfloat16)
    grad_down_part = matmul_tn(hidden_low, grad_out_low)
    grad_outb_mlp = jnp.sum(grad_out_rows, axis=0)
    grad_hidden = matmul_nt(grad_out_low, down_proj)
    grad_pre_low = gelu_back(grad_hidden)[0].astype(jnp.bfloat16)
    grad_up_part = matmul_tn(normed2_low, grad_pre_low)
    grad_upb_part = jnp.sum(grad_pre_low.astype(jnp.float32), axis=0)
    grad_normed2 = matmul_nt(grad_pre_low, up_proj)
    grad_mid_part, grad_gain_mlp, grad_shift_mlp = ln2_back(grad_normed2)
    grad_middle = grad_out_rows + grad_mid_part
    grad_branch = grad_middle.astype(jnp.bfloat16)
    grad_outp_part = matmul_tn(mixed_low, grad_branch)
    grad_outb_attn = jnp.sum(grad_branch.astype(jnp.float32), axis=0)
    grad_mixed_low = matmul_nt(grad_branch, out_proj).astype(jnp.bfloat16)
    grad_mixed3 = grad_mixed_low.reshape(slots, clips, width)

    def query_side(number):
        offset = number * lane_width
        query_pair = head_pair(query3, offset, lane_width, DH)
        grad_pair = head_pair(grad_mixed3, offset, lane_width, DH)
        key_pair = head_pair(all_memory, offset, lane_width, DH)
        value_pair = head_pair(all_memory, width + offset, lane_width, DH)
        log_pair = lax.dynamic_slice_in_dim(log_rows, 2 * number, 2, 2)
        probability = pair_probs(query_pair, key_pair, log_pair, key_mask, scale)
        grad_probs = jnp.einsum(
            "qchd,kchd->chqk", grad_pair, value_pair, preferred_element_type=jnp.float32
        )
        delta = jnp.sum(probability * grad_probs, axis=-1, keepdims=True)
        grad_scores = (probability * (grad_probs - delta)).astype(jnp.bfloat16)
        grad_query = (
            jnp.einsum("chqk,kchd->qchd", grad_scores, key_pair, preferred_element_type=jnp.float32)
            * scale
        )
        return (
            offset,
            query_pair,
            grad_pair,
            probability,
            grad_scores,
            delta,
            grad_query.reshape(slots, clips, lane_width),
        )

    zero_query = jnp.zeros((slots, clips, width), jnp.float32)

    def backward_pair(number, state):
        grad_query_acc, grad_memory = state
        side = query_side(number)
        offset = side[0]
        grad_keys = (
            jnp.einsum("chqk,qchd->kchd", side[4], side[1], preferred_element_type=jnp.float32)
            * scale
        )
        grad_values = jnp.einsum(
            "chqk,qchd->kchd",
            side[3].astype(jnp.bfloat16),
            side[2],
            preferred_element_type=jnp.float32,
        )
        grad_memory = add_lanes(
            grad_memory, grad_keys.reshape(key_count, clips, lane_width), offset
        )
        grad_memory = add_lanes(
            grad_memory, grad_values.reshape(key_count, clips, lane_width), width + offset
        )
        return (add_lanes(grad_query_acc, side[6], offset), grad_memory)

    grad_query_full, grad_memory_all = lax.fori_loop(
        0,
        pair_count,
        backward_pair,
        (zero_query, jnp.zeros((key_count, clips, 2 * width), jnp.float32)),
    )
    grad_memory_own = lax.psum_scatter(
        grad_memory_all, ("freq", "tm"), scatter_dimension=0, tiled=True
    )
    grad_query_low = grad_query_full.reshape(row_count, width).astype(jnp.bfloat16)
    grad_memory_low = grad_memory_own.reshape(row_count, 2 * width).astype(jnp.bfloat16)
    grad_joint = jnp.concatenate([grad_query_low, grad_memory_low], axis=1)
    grad_joint_part = matmul_tn(normed1_low, grad_joint)
    grad_bias_cols = jnp.stack(
        [
            jnp.sum(grad_query_low.astype(jnp.float32), axis=0),
            jnp.sum(grad_memory_low[:, width:].astype(jnp.float32), axis=0),
        ],
        axis=1,
    )
    grad_normed1 = matmul_nt(grad_joint, joint_proj)
    grad_in_part, grad_gain_attn, grad_shift_attn = ln1_back(grad_normed1)
    grad_patches = (grad_middle + grad_in_part).astype(jnp.bfloat16).reshape(slots, clips, width)
    shares = (
        lax.psum_scatter(
            grad_joint_part.astype(jnp.bfloat16), ("freq", "tm"), scatter_dimension=0, tiled=True
        ).astype(jnp.float32),
        lax.psum_scatter(
            grad_bias_cols.astype(jnp.bfloat16), ("freq", "tm"), scatter_dimension=0, tiled=True
        ).astype(jnp.float32),
        lax.psum_scatter(
            grad_outp_part.astype(jnp.bfloat16), ("freq", "tm"), scatter_dimension=0, tiled=True
        ).astype(jnp.float32),
        lax.psum_scatter(
            grad_outb_attn.astype(jnp.bfloat16), ("freq", "tm"), scatter_dimension=0, tiled=True
        ).astype(jnp.float32),
        lax.psum_scatter(
            grad_gain_attn.astype(jnp.bfloat16), ("freq", "tm"), scatter_dimension=0, tiled=True
        ).astype(jnp.float32),
        lax.psum_scatter(
            grad_shift_attn.astype(jnp.bfloat16), ("freq", "tm"), scatter_dimension=0, tiled=True
        ).astype(jnp.float32),
        lax.psum_scatter(
            grad_up_part.astype(jnp.bfloat16), ("freq", "tm"), scatter_dimension=0, tiled=True
        ).astype(jnp.float32),
        lax.psum_scatter(
            grad_upb_part.astype(jnp.bfloat16), ("freq", "tm"), scatter_dimension=0, tiled=True
        ).astype(jnp.float32),
        lax.psum_scatter(
            grad_down_part.astype(jnp.bfloat16), ("freq", "tm"), scatter_dimension=0, tiled=True
        ).astype(jnp.float32),
        lax.psum_scatter(
            grad_outb_mlp.astype(jnp.bfloat16), ("freq", "tm"), scatter_dimension=0, tiled=True
        ).astype(jnp.float32),
        lax.psum_scatter(
            grad_gain_mlp.astype(jnp.bfloat16), ("freq", "tm"), scatter_dimension=0, tiled=True
        ).astype(jnp.float32),
        lax.psum_scatter(
            grad_shift_mlp.astype(jnp.bfloat16), ("freq", "tm"), scatter_dimension=0, tiled=True
        ).astype(jnp.float32),
    )
    summed_all = (
        lax.psum(shares[0].astype(jnp.bfloat16), "dp").astype(jnp.float32),
        lax.psum(shares[1].astype(jnp.bfloat16), "dp").astype(jnp.float32),
        lax.psum(shares[2].astype(jnp.bfloat16), "dp").astype(jnp.float32),
        lax.psum(shares[3].astype(jnp.bfloat16), "dp").astype(jnp.float32),
        lax.psum(shares[4].astype(jnp.bfloat16), "dp").astype(jnp.float32),
        lax.psum(shares[5].astype(jnp.bfloat16), "dp").astype(jnp.float32),
        lax.psum(shares[6].astype(jnp.bfloat16), "dp").astype(jnp.float32),
        lax.psum(shares[7].astype(jnp.bfloat16), "dp").astype(jnp.float32),
        lax.psum(shares[8].astype(jnp.bfloat16), "dp").astype(jnp.float32),
        lax.psum(shares[9].astype(jnp.bfloat16), "dp").astype(jnp.float32),
        lax.psum(shares[10].astype(jnp.bfloat16), "dp").astype(jnp.float32),
        lax.psum(shares[11].astype(jnp.bfloat16), "dp").astype(jnp.float32),
    )
    attn_summed = summed_all[:6]
    mlp_summed = summed_all[6:]
    grad_norm_gain = jnp.stack([attn_summed[4], mlp_summed[4]])
    grad_norm_shift = jnp.stack([attn_summed[5], mlp_summed[5]])
    grad_out_bias = jnp.stack([attn_summed[3], mlp_summed[3]])
    grad_proj_bias = jnp.transpose(attn_summed[1])
    return (
        output,
        grad_patches,
        grad_norm_gain,
        grad_norm_shift,
        attn_summed[0],
        grad_proj_bias,
        attn_summed[2],
        mlp_summed[0],
        mlp_summed[1],
        mlp_summed[2],
        grad_out_bias,
    )


def solution(mesh):
    return jax.shard_map(
        per_device,
        mesh=mesh,
        in_specs=(
            P(("freq", "tm"), "dp", None),
            P(),
            P(),
            P(),
            P(),
            P(),
            P(),
            P(),
            P(),
            P(),
            P(),
            P(("freq", "tm"), "dp", None),
        ),
        out_specs=(
            P(("freq", "tm"), "dp", None),
            P(("freq", "tm"), "dp", None),
            P(None, ("freq", "tm")),
            P(None, ("freq", "tm")),
            P(("freq", "tm"), None),
            P(None, ("freq", "tm")),
            P(("freq", "tm"), None),
            P(("freq", "tm"), None),
            P(("freq", "tm")),
            P(("freq", "tm"), None),
            P(None, ("freq", "tm")),
        ),
        check_vma=False,
    )
```

profile of v0, /device:TPU:0, one launch (start us, length us, event | category | flops | bytes accessed | tf_op | source)
XLA Modules:
  0.0 1731.1 jit_solution(16705769092683540999)
XLA Ops:
  18.8 6.9 fusion.65
  36.0 4.9 copy.43
  44.3 144.5 %all-gather.2.cloned.1.call-done = bf16[1312,8,1536]{2,1,0:T(8,128)(2,1)} async-done(((bf16[164,8,1536]{2,1,0:T(8,128)(2,1)}), bf16[1312,8,1536]{2,1,0:T(8,128)(2,1)}) %all-gather.2.cloned.1.call-update) | async-done | bytes 32243728 | tf_op jit(solution)/shard_map/all_gather | solution.py:133
  188.8 42.4 %copy.42 = bf16[1312,8,1536]{0,2,1:T(8,128)(2,1)} copy(bf16[1312,8,1536]{2,1,0:T(8,128)(2,1)} %all-gather.2.cloned.1.call-done) | data formatting | bytes 64487424 | tf_op jit(solution)/shard_map/while | solution.py:160
  231.9 122.6 %while.34 = (s32[]{:T(128)}, bf16[164,8,768]{2,1,0:T(8,128)(2,1)}, f32[164,8,12]{0,2,1:T(8,128)}, bf16[1312,8,1536]{0,2,1:T(8,128)(2,1)}, bf16[164,8,768]{0,2,1:...) while((s32[]{:T(128)}, bf16[164,8,768]{2,1,0:T(8,128)(2,1)}, ...), condition=%wide.region_6.7_spmd, body=%wide.region_3.6_spmd.sunk | while | flops 922637760 | bytes 60295916 | solution.py:160
  242.2 5.1 fusion.126
  262.6 5.1 fusion.126
  283.0 5.1 fusion.126
  303.5 5.1 fusion.126
  323.9 5.1 fusion.126
  344.3 5.1 fusion.126
  354.5 4.6 fusion.74
  360.4 45.8 %multiply_convert_fusion.1 = (bf16[1312,3072]{1,0:T(8,128)(2,1)}, f32[1312,3072]{1,0:T(8,128)}, f32[1312,3072]{1,0:T(8,128)}) fusion(f32[3072]{0:T(1024)S(1)} %copy-done.41, bf16[768,3072]{1,0:T(8,128)(2,1)S(1)} %bitcast.204, f32[1312,768]{1,0:T(8,128)S(1)} %get-tuple-element.504, f32[768]{0:T(1024)S(1)} %copy-done.46, f32[768]{0:T(1024)S(1)} %copy-done.39, ...), kind=kOutput, calls=%fused_computation.34 | convolution fusion | flops 6461841408 | bytes 49082624 | tf_op jit(solution)/shard_map/dot_general | solution.py:36
  406.3 21.5 %fusion.75 = (bf16[3072]{0:T(1024)(128)(2,1)}, bf16[1312,3072]{1,0:T(8,128)(2,1)}) fusion(f32[1312,3072]{1,0:T(8,128)} %get-tuple-element.492, bf16[3072,768]{1,0:T(8,128)(2,1)} %param.25, bf16[164,8,768]{2,1,0:T(8,128)(2,1)} %param.27, f32[1312]{0:T(1024)S(1)} %copy-done.22, f32[1312,3072]{1,0:T(8,128)} %get-tuple-element.505, f32[3072]{0:T(1024)} %convert_element_type.229), kind=kOutput, calls=%fused_computation.178 | convolution fusion | flops 6258299904 | bytes 47062144 | tf_op jit(solution)/shard_map/dot_general | solution.py:46
  427.8 14.1 multiply_reduce_fusion.1
  451.1 21.7 %broadcast_in_dim.96 = f32[1312,8,1536]{0,2,1:T(8,128)} broadcast(f32[]{:T(128)} %constant.301.clone.1), dimensions={} | broadcast | bytes 64487428 | tf_op jit(solution)/shard_map/broadcast_in_dim | solution.py:250
  472.7 478.7 %while.35 = (s32[]{:T(128)}, f32[164,8,768]{2,1,0:T(8,128)}, f32[1312,8,1536]{0,2,1:T(8,128)}, bf16[1312,8,1536]{0,2,1:T(8,128)(2,1)}, bf16[164,8,768]{0,2,1:T(8...) while((s32[]{:T(128)}, f32[164,8,768]{2,1,0:T(8,128)}, ...), condition=%wide.region_14.15_spmd, body=%wide.region_12.14_spmd.sunk | while | flops 2238668288 | bytes 267073456 | solution.py:246
  487.8 7.6 fusion.137
  495.4 11.0 multiply_reduce_fusion.5
  506.5 10.5 multiply_convert_fusion.4
  539.5 7.5 constant_dynamic-update-slice_fusion.10
  547.1 5.7 constant_dynamic-update-slice_fusion.11
  567.5 7.6 fusion.137
  575.2 11.0 multiply_reduce_fusion.5
  586.2 10.5 multiply_convert_fusion.4
  619.3 7.5 constant_dynamic-update-slice_fusion.10
  626.9 5.7 constant_dynamic-update-slice_fusion.11
  647.3 7.6 fusion.137
  655.0 11.0 multiply_reduce_fusion.5
  666.0 10.5 multiply_convert_fusion.4
  699.2 7.5 constant_dynamic-update-slice_fusion.10
  706.6 5.6 constant_dynamic-update-slice_fusion.11
  727.1 7.6 fusion.137
  734.7 11.0 multiply_reduce_fusion.5
  745.8 10.5 multiply_convert_fusion.4
  778.8 7.5 constant_dynamic-update-slice_fusion.10
  786.3 5.6 constant_dynamic-update-slice_fusion.11
  806.8 7.6 fusion.137
  814.4 11.0 multiply_reduce_fusion.5
  825.5 10.5 multiply_convert_fusion.4
  858.5 7.5 constant_dynamic-update-slice_fusion.10
  866.0 5.7 constant_dynamic-update-slice_fusion.11
  886.4 7.6 fusion.137
  894.1 11.0 multiply_reduce_fusion.5
  905.2 10.5 multiply_convert_fusion.4
  938.3 7.5 constant_dynamic-update-slice_fusion.10
  945.8 5.7 constant_dynamic-update-slice_fusion.11
  951.5 67.9 %copy.49 = f32[1312,8,1536]{2,1,0:T(8,128)} copy(f32[1312,8,1536]{0,2,1:T(8,128)} %get-tuple-element.368) | data formatting | bytes 128974848 | tf_op jit(solution)/shard_map/while | solution.py:246
  1019.5 5.2 fusion.41
  1024.8 12.6 convolution_convert_fusion.2
  1038.1 15.0 convolution_convert_fusion.1
  1057.5 334.1 %reduce-scatter.9.cloned.1.call-done = f32[164,8,1536]{2,1,0:T(8,128)} async-done(((f32[1312,8,1536]{2,1,0:T(8,128)}), f32[164,8,1536]{2,1,0:T(8,128)}) %reduce-scatter.9.cloned.1.call-update) | async-done | bytes 8060944 | tf_op jit(solution)/shard_map/reduce_scatter | solution.py:252
  1397.5 8.9 convolution_convert_fusion
  1414.3 11.5 fusion.40
  1428.3 11.0 fusion.69
  1440.2 5.6 fusion.21
  1445.8 27.6 %all-reduce.7 = (bf16[768]{0:T(1024)(128)(2,1)}, bf16[768]{0:T(1024)(128)(2,1)}, bf16[768]{0:T(1024)(128)(2,1)}, bf16[768]{0:T(1024)(128)(2,1)}, bf16[3072]{0:T(...) all-reduce(bf16[768]{0:T(1024)(128)(2,1)} %get-tuple-element.425, ...), channel_id=4, replica_groups=mesh['dp'=4,'freq'=2,'tm'=4] {'freq','tm'}, use_global_device_ids=true, to_apply=%region_22.23.clone | all-reduce | flops 7680 | bytes 30720
  1474.6 15.7 reduce-scatter.17.cloned.1.call-done
  1490.3 57.2 %reduce-scatter.15.cloned.1.call-done = bf16[96,3072]{1,0:T(8,128)(2,1)} async-done(((bf16[768,3072]{1,0:T(8,128)(2,1)}), bf16[96,3072]{1,0:T(8,128)(2,1)}) %reduce-scatter.15.cloned.1.call-update) | async-done | bytes 589840 | tf_op jit(solution)/shard_map/reduce_scatter | solution.py:288
  1547.5 51.8 %reduce-scatter.11.cloned.1.call-done = bf16[96,2304]{1,0:T(8,128)(2,1)} async-done(((bf16[768,2304]{1,0:T(8,128)(2,1)}), bf16[96,2304]{1,0:T(8,128)(2,1)}) %reduce-scatter.11.cloned.1.call-update) | async-done | bytes 442384 | tf_op jit(solution)/shard_map/reduce_scatter | solution.py:270
  1607.7 6.7 fusion.34
  1614.4 22.4 %reduce-scatter.19.cloned.1.call-done = bf16[96,2]{1,0:T(8,128)(2,1)} async-done(((bf16[768,2]{1,0:T(8,128)(2,1)}), bf16[96,2]{1,0:T(8,128)(2,1)}) %reduce-scatter.19.cloned.1.call-update) | async-done | bytes 400
  1637.6 12.7 all-reduce.8
  1655.2 60.9 %all-reduce.12.cloned.1.call-done = (bf16[96,2304]{1,0:T(8,128)(2,1)}, bf16[96,768]{1,0:T(8,128)(2,1)}, bf16[96,3072]{1,0:T(8,128)(2,1)}, bf16[384,768]{1,0:T(8,128)(2,1)}) async-done(((bf16[96,2304]{1,0:T(8,128)(2,1)}, bf16[96,768]{1,0:T(8,128)(2,1)}, bf16[96,3072]{1,0:T(8,128)(2,1)}, bf16[384,768]{1,0:T(8,128)(2,1)}), (bf16[96,2304]{1,0:T(8,128)(2,1)}, bf16[96,768]{1,0:T(8,128)(2,1)}, ...) | async-done | bytes 1769488 | tf_op jit(solution)/shard_map/psum | solution.py:308
  (420 shorter events, 396.5 us)
Async XLA Ops:
  7.2 11.6 copy-start
  7.2 6.0 copy-start.48
  7.2 6.6 copy-start.49
  7.2 181.6 %all-gather.2.cloned.1.call-start = ((), (), s32[]{:S(2)}) async-start(), calls=%async_computation.6 | async-start | bytes 36274176 | tf_op jit(solution)/shard_map/all_gather | solution.py:133
  10.9 14.7 copy-start.20
  17.4 8.3 copy-start.29
  17.4 8.3 copy-start.24
  18.8 6.9 copy-start.33
  18.8 6.9 copy-start.44
  30.7 1360.9 %reduce-scatter.9.cloned.1.call-start = ((), (), s32[]{:S(2)}) async-start(), calls=%async_computation.7 | async-start | bytes 72548352 | tf_op jit(solution)/shard_map/reduce_scatter | solution.py:252
  359.1 47.1 %copy-start.9 = (f32[1312,768]{1,0:T(8,128)}, f32[1312,768]{1,0:T(8,128)S(1)}, u32[]{:S(2)}) copy-start(f32[1312,768]{1,0:T(8,128)S(1)} %get-tuple-element.504) | copy-start | bytes 12091396
  359.2 82.8 %copy-start.31 = (f32[1312]{0:T(1024)}, f32[1312]{0:T(1024)S(1)}, u32[]{:S(2)}) copy-start(f32[1312]{0:T(1024)S(1)} %broadcast_multiply_fusion.1) | copy-start | bytes 15748
  359.8 46.5 %copy-start.35 = (f32[1312]{0:T(1024)}, f32[1312]{0:T(1024)S(1)}, u32[]{:S(2)}) copy-start(f32[1312]{0:T(1024)S(1)} %fusion.60) | copy-start | bytes 15748
  360.4 45.9 %copy-start.22 = (f32[1312]{0:T(1024)S(1)}, f32[1312]{0:T(1024)}, u32[]{:S(2)}) copy-start(f32[1312]{0:T(1024)} %convert_element_type.232) | copy-start | bytes 15748
  427.8 14.1 copy-start.28
  427.8 14.2 copy-start.10
  427.8 14.2 copy-start.36
  427.8 14.2 copy-start.40
  451.1 21.7 %copy-start.15 = (f32[1312]{0:T(1024)S(1)}, f32[1312]{0:T(1024)}, u32[]{:S(2)}) copy-start(f32[1312]{0:T(1024)} %get-tuple-element.731) | copy-start | bytes 15748
  487.7 18.7 %copy-start.2 = (bf16[1312,8,128]{0,2,1:T(8,128)(2,1)}, bf16[1312,8,128]{0,2,1:T(8,128)(2,1)S(1)}, u32[]{:S(2)}) copy-start(bf16[1312,8,128]{0,2,1:T(8,128)(2,1)S(1)} %get-tuple-element.610) | copy-start | bytes 8060932 | tf_op jit(solution)/shard_map/while
  487.7 7.7 copy-start.4
  487.7 7.7 copy-start.19
  506.5 14.0 copy-start.1
  537.3 9.7 slice-start
  539.5 7.5 slice-start.1
  567.5 18.7 %copy-start.2 = (bf16[1312,8,128]{0,2,1:T(8,128)(2,1)}, bf16[1312,8,128]{0,2,1:T(8,128)(2,1)S(1)}, u32[]{:S(2)}) copy-start(bf16[1312,8,128]{0,2,1:T(8,128)(2,1)S(1)} %get-tuple-element.610) | copy-start | bytes 8060932 | tf_op jit(solution)/shard_map/while
  567.5 7.7 copy-start.4
  567.5 7.7 copy-start.19
  586.2 14.0 copy-start.1
  617.1 9.8 slice-start
  619.3 7.6 slice-start.1
  647.3 18.7 %copy-start.2 = (bf16[1312,8,128]{0,2,1:T(8,128)(2,1)}, bf16[1312,8,128]{0,2,1:T(8,128)(2,1)S(1)}, u32[]{:S(2)}) copy-start(bf16[1312,8,128]{0,2,1:T(8,128)(2,1)S(1)} %get-tuple-element.610) | copy-start | bytes 8060932 | tf_op jit(solution)/shard_map/while
  647.3 7.7 copy-start.4
  647.3 7.7 copy-start.19
  666.0 14.0 copy-start.1
  696.9 9.7 slice-start
  699.1 7.5 slice-start.1
  727.0 18.7 %copy-start.2 = (bf16[1312,8,128]{0,2,1:T(8,128)(2,1)}, bf16[1312,8,128]{0,2,1:T(8,128)(2,1)S(1)}, u32[]{:S(2)}) copy-start(bf16[1312,8,128]{0,2,1:T(8,128)(2,1)S(1)} %get-tuple-element.610) | copy-start | bytes 8060932 | tf_op jit(solution)/shard_map/while
  727.0 7.7 copy-start.4
  727.1 7.7 copy-start.19
  745.8 14.0 copy-start.1
  776.6 9.7 slice-start
  778.8 7.5 slice-start.1
  806.7 18.7 %copy-start.2 = (bf16[1312,8,128]{0,2,1:T(8,128)(2,1)}, bf16[1312,8,128]{0,2,1:T(8,128)(2,1)S(1)}, u32[]{:S(2)}) copy-start(bf16[1312,8,128]{0,2,1:T(8,128)(2,1)S(1)} %get-tuple-element.610) | copy-start | bytes 8060932 | tf_op jit(solution)/shard_map/while
  806.7 7.7 copy-start.4
  806.7 7.7 copy-start.19
  825.5 14.0 copy-start.1
  856.3 9.7 slice-start
  858.5 7.5 slice-start.1
  886.4 18.7 %copy-start.2 = (bf16[1312,8,128]{0,2,1:T(8,128)(2,1)}, bf16[1312,8,128]{0,2,1:T(8,128)(2,1)S(1)}, u32[]{:S(2)}) copy-start(bf16[1312,8,128]{0,2,1:T(8,128)(2,1)S(1)} %get-tuple-element.610) | copy-start | bytes 8060932 | tf_op jit(solution)/shard_map/while
  886.4 7.7 copy-start.4
  886.4 7.7 copy-start.19
  905.1 14.0 copy-start.1
  936.0 9.8 slice-start
  938.3 7.5 slice-start.1
  1019.4 455.2 %reduce-scatter.13.cloned.1.call-start = ((), (), s32[]{:S(2)}) async-start(), calls=%async_computation.9 | async-start | bytes 1327104 | tf_op jit(solution)/shard_map/reduce_scatter | solution.py:276
  1024.7 465.6 %reduce-scatter.17.cloned.1.call-start = ((), (), s32[]{:S(2)}) async-start(), calls=%async_computation.11 | async-start | bytes 5308416 | tf_op jit(solution)/shard_map/reduce_scatter | solution.py:294
  1037.4 510.0 %reduce-scatter.15.cloned.1.call-start = ((), (), s32[]{:S(2)}) async-start(), calls=%async_computation.10 | async-start | bytes 5308416 | tf_op jit(solution)/shard_map/reduce_scatter | solution.py:288
  1053.1 546.2 %reduce-scatter.11.cloned.1.call-start = ((), (), s32[]{:S(2)}) async-start(), calls=%async_computation.8 | async-start | bytes 3981312 | tf_op jit(solution)/shard_map/reduce_scatter | solution.py:270
  1057.5 340.0 %copy-start.21 = (f32[1312]{0:T(1024)S(1)}, f32[1312]{0:T(1024)}, u32[]{:S(2)}) copy-start(f32[1312]{0:T(1024)} %copy-done.20) | copy-start | bytes 15748
  1406.4 230.3 %reduce-scatter.19.cloned.1.call-start = ((), (), s32[]{:S(2)}) async-start(), calls=%async_computation.12 | async-start | bytes 221184
  1414.3 11.5 copy-start.13
  1428.3 11.0 copy-start.30
  1440.0 276.1 %all-reduce.12.cloned.1.call-start = ((), (), s32[]{:S(2)}) async-start(), calls=%async_computation.13 | async-start | bytes 3538944 | tf_op jit(solution)/shard_map/psum | solution.py:308
  (49 other events, 173.5 us)
Sparse Core Ops, SparseCore 0:
  30.8 157.9 all-gather.1
  1019.5 372.0 reduce-scatter.8
  1395.4 36.7 reduce-scatter.12
  1435.9 54.3 reduce-scatter.16
  1493.6 53.8 reduce-scatter.14
  1551.2 48.0 reduce-scatter.10
  1603.2 33.4 reduce-scatter.18
  1639.4 76.6 all-reduce.11
where the time goes:
time: 1740 us; the launch traced here: 1730 us
  waiting for transfers between devices  687 us (39%)
  matrix products  398 us (23%)
  local copies, waits for them, and re-layouts  349 us (20%)
  other arithmetic  239 us (14%)
  blocking collectives  40.3 us (2%)
    reduce_scatter x1, waiting for transfers between devices, per_device(): lax.psum_scatter(grad_memory_all, ('freq', 'tm'), scatter_dimension=0, ti...  334 us
    all_gather x1, waiting for transfers between devices, per_device(): all_memory = lax.all_gather(key_value, ('freq', 'tm'), axis=0, tiled=True)  144 us
    dynamic_update_slice x12, other arithmetic, add_lanes(): return lax.dynamic_update_slice_in_dim(target, current + addend, offset, 2)  78.9 us
    dynamic_slice x36, local copies, waits for them, and re-layouts, head_pair(): section = lax.dynamic_slice_in_dim(array, offset, lane_width, 2)  78.8 us
    dot_general x4, matrix products, matmul(): return jnp.dot(left, right, preferred_element_type=jnp.float32)  68.8 us
    while x1, local copies, waits for them, and re-layouts, per_device(): lax.fori_loop(0, pair_count, backward_pair, (zero_query, jnp.zeros((key_c...  67.9 us
    dot_general x6, matrix products, pair_probs(): jnp.einsum('qchd,kchd->chqk', query_pair, key_pair, preferred_element_typ...  66.2 us
    convert_element_type x6, other arithmetic, query_side(): grad_scores = (probability * (grad_probs - delta)).astype(jnp.bfloat16)  62.9 us
  transfers between devices with their start and end apart: 8, of which 7 were waited for; matrix products, arithmetic and copies ran while one was open for 7% of the time, Pallas kernels for 0%

commit v1 on v0

--- a/solution.py
+++ b/solution.py
@@ -130,7 +130,18 @@
     memory_low = (joint[:, 2 * width :] + bias_full[1]).astype(jnp.bfloat16)
     query3 = query_low.reshape(slots, clips, width)
     key_value = jnp.concatenate([keys_low, memory_low], axis=1).reshape(slots, clips, 2 * width)
-    all_memory = lax.all_gather(key_value, ("freq", "tm"), axis=0, tiled=True)
+    ways = lax.axis_size(("freq", "tm"))
+    up = [(d, (d + 1) % ways) for d in range(ways)]
+    down = [(d, (d - 1) % ways) for d in range(ways)]
+    earlier, later = ([key_value], [key_value])
+    for _ in range(ways // 2):
+        earlier.append(lax.ppermute(earlier[-1], ("freq", "tm"), up))
+    for _ in range((ways - 1) // 2):
+        later.append(lax.ppermute(later[-1], ("freq", "tm"), down))
+    line = jnp.concatenate([*earlier[::-1], *later[1:]], axis=0)
+    all_memory = jnp.roll(
+        line, (lax.axis_index(("freq", "tm")) - ways // 2) * key_value.shape[0], axis=0
+    )
 
     def forward_pair(number, state):
         mixed_acc, log_acc = state

time: 1740 us -> 2250 us (1.29)
  waiting for transfers between devices: 687 us -> 1100 us
  local copies, waits for them, and re-layouts: 349 us -> 429 us
    ppermute x0 -> x7, waiting for transfers between devices: none -> 560 us  [the longest x4 326 us: per_device(): earlier.append(lax.ppermute(earlier[-1], ('freq', 'tm'), up))]
    all_gather x1 -> x0, waiting for transfers between devices: 144 us -> none  [per_device(): all_memory = lax.all_gather(key_value, ('freq', 'tm'), axis=0, tiled=True)]
    unnamed x94 -> x127, local copies, waits for them, and re-layouts: 9.75 us -> 63 us
  transfers between devices with their start and end apart: 8 -> 14, of which waited for: 7 -> 13; matrix products, arithmetic and copies ran while one was open for 7% -> 6% of each run, Pallas kernels for 0% -> 0%
where the time goes in v1:
time: 2250 us; the launch traced here: 2240 us
  waiting for transfers between devices  1100 us (49%)
  local copies, waits for them, and re-layouts  429 us (19%)
  matrix products  397 us (18%)
  other arithmetic  242 us (11%)
  blocking collectives  40.4 us (2%)
    reduce_scatter x1, waiting for transfers between devices, per_device(): lax.psum_scatter(grad_memory_all, ('freq', 'tm'), scatter_dimension=0, ti...  335 us
    ppermute x4, waiting for transfers between devices, per_device(): earlier.append(lax.ppermute(earlier[-1], ('freq', 'tm'), up))  326 us
    ppermute x3, waiting for transfers between devices, per_device(): later.append(lax.ppermute(later[-1], ('freq', 'tm'), down))  234 us
    dynamic_update_slice x12, other arithmetic, add_lanes(): return lax.dynamic_update_slice_in_dim(target, current + addend, offset, 2)  78.9 us
    dynamic_slice x36, local copies, waits for them, and re-layouts, head_pair(): section = lax.dynamic_slice_in_dim(array, offset, lane_width, 2)  78.8 us
    dot_general x4, matrix products, matmul(): return jnp.dot(left, right, preferred_element_type=jnp.float32)  68.2 us
    while x1, local copies, waits for them, and re-layouts, per_device(): lax.fori_loop(0, pair_count, backward_pair, (zero_query, jnp.zeros((key_c...  67.7 us
    dot_general x6, matrix products, pair_probs(): jnp.einsum('qchd,kchd->chqk', query_pair, key_pair, preferred_element_typ...  66.2 us
  transfers between devices with their start and end apart: 14, of which 13 were waited for; matrix products, arithmetic and copies ran while one was open for 6% of the time, Pallas kernels for 0%

profile of v1, /device:TPU:0, one launch (start us, length us, event | category | flops | bytes accessed | tf_op | source)
XLA Modules:
  0.0 2240.2 jit_solution(2833543960884133687)
XLA Ops:
  19.4 6.9 fusion.65
  33.3 87.2 %collective-permute-done = bf16[164,8,1536]{2,1,0:T(8,128)(2,1)S(1)} collective-permute-done((bf16[164,8,1536]{2,1,0:T(8,128)(2,1)S(1)}, bf16[164,8,1536]{2,1,0:T(8,128)(2,1)S(1)}, u32[]{:S(2)}, u32[]{:S(2)}) %collective-permute-start) | collective-permute-done | bytes 4030496 | tf_op jit(solution)/shard_map/ppermute | solution.py:138
  125.0 86.8 %collective-permute-done.1 = bf16[164,8,1536]{2,1,0:T(8,128)(2,1)S(1)} collective-permute-done((bf16[164,8,1536]{2,1,0:T(8,128)(2,1)S(1)}, bf16[164,8,1536]{2,1,0:T(8,128)(2,1)S(1)}, u32[]{:S(2)}, u32[]{:S(2)}) %collective-permute-start.1) | collective-permute-done | bytes 4030496 | tf_op jit(solution)/shard_map/ppermute | solution.py:138
  214.0 86.7 %collective-permute-done.4 = bf16[164,8,1536]{2,1,0:T(8,128)(2,1)S(1)} collective-permute-done((bf16[164,8,1536]{2,1,0:T(8,128)(2,1)S(1)}, bf16[164,8,1536]{2,1,0:T(8,128)(2,1)S(1)}, u32[]{:S(2)}, u32[]{:S(2)}) %collective-permute-start.4) | collective-permute-done | bytes 4030496 | tf_op jit(solution)/shard_map/ppermute | solution.py:140
  302.7 82.0 %collective-permute-done.2 = bf16[164,8,1536]{2,1,0:T(8,128)(2,1)} collective-permute-done((bf16[164,8,1536]{2,1,0:T(8,128)(2,1)S(1)}, bf16[164,8,1536]{2,1,0:T(8,128)(2,1)}, u32[]{:S(2)}, u32[]{:S(2)}) %collective-permute-start.2) | collective-permute-done | bytes 4030496 | tf_op jit(solution)/shard_map/ppermute | solution.py:138
  386.9 86.7 %collective-permute-done.5 = bf16[164,8,1536]{2,1,0:T(8,128)(2,1)} collective-permute-done((bf16[164,8,1536]{2,1,0:T(8,128)(2,1)S(1)}, bf16[164,8,1536]{2,1,0:T(8,128)(2,1)}, u32[]{:S(2)}, u32[]{:S(2)}) %collective-permute-start.5) | collective-permute-done | bytes 4030496 | tf_op jit(solution)/shard_map/ppermute | solution.py:140
  487.4 70.0 %collective-permute-done.3 = bf16[164,8,1536]{2,1,0:T(8,128)(2,1)} collective-permute-done((bf16[164,8,1536]{2,1,0:T(8,128)(2,1)}, bf16[164,8,1536]{2,1,0:T(8,128)(2,1)}, u32[]{:S(2)}, u32[]{:S(2)}) %collective-permute-start.3) | collective-permute-done | bytes 4030496 | tf_op jit(solution)/shard_map/ppermute | solution.py:138
  583.6 60.6 %collective-permute-done.6 = bf16[164,8,1536]{2,1,0:T(8,128)(2,1)} collective-permute-done((bf16[164,8,1536]{2,1,0:T(8,128)(2,1)}, bf16[164,8,1536]{2,1,0:T(8,128)(2,1)}, u32[]{:S(2)}, u32[]{:S(2)}) %collective-permute-start.6) | collective-permute-done | bytes 4030496 | tf_op jit(solution)/shard_map/ppermute | solution.py:140
  675.0 22.1 constant_dynamic-slice_fusion.8
  697.1 42.4 %copy.48 = bf16[1312,8,1536]{0,2,1:T(8,128)(2,1)} copy(bf16[1312,8,1536]{2,1,0:T(8,128)(2,1)} %constant_dynamic-slice_fusion.8) | data formatting | bytes 64487424 | tf_op jit(solution)/shard_map/while | solution.py:171
  740.2 122.8 %while.34 = (s32[]{:T(128)}, bf16[164,8,768]{2,1,0:T(8,128)(2,1)}, f32[164,8,12]{0,2,1:T(8,128)}, bf16[1312,8,1536]{0,2,1:T(8,128)(2,1)}, bf16[164,8,768]{0,2,1:...) while((s32[]{:T(128)}, bf16[164,8,768]{2,1,0:T(8,128)(2,1)}, ...), condition=%wide.region_6.7_spmd, body=%wide.region_3.6_spmd.sunk | while | flops 922637760 | bytes 60295916 | solution.py:171
  750.5 5.1 fusion.126
  868.9 45.3 %multiply_convert_fusion.1 = (bf16[1312,3072]{1,0:T(8,128)(2,1)}, f32[1312,3072]{1,0:T(8,128)}, f32[1312,3072]{1,0:T(8,128)}) fusion(f32[3072]{0:T(1024)S(1)} %copy-done.51, bf16[768,3072]{1,0:T(8,128)(2,1)S(1)} %bitcast.208, f32[1312,768]{1,0:T(8,128)S(1)} %get-tuple-element.504, f32[768]{0:T(1024)S(1)} %copy-done.56, f32[768]{0:T(1024)S(1)} %copy-done.49, ...), kind=kOutput, calls=%fused_computation.34 | convolution fusion | flops 6461841408 | bytes 49082624 | tf_op jit(solution)/shard_map/dot_general | solution.py:36
  914.2 21.6 fusion.75
  935.8 14.1 multiply_reduce_fusion.1
  959.1 21.7 broadcast_in_dim.96
  980.8 478.8 %while.35 = (s32[]{:T(128)}, f32[164,8,768]{2,1,0:T(8,128)}, f32[1312,8,1536]{0,2,1:T(8,128)}, bf16[1312,8,1536]{0,2,1:T(8,128)(2,1)}, bf16[164,8,768]{0,2,1:T(8...) while((s32[]{:T(128)}, f32[164,8,768]{2,1,0:T(8,128)}, ...), condition=%wide.region_14.15_spmd, body=%wide.region_12.14_spmd.sunk | while | flops 2238668288 | bytes 267073456 | solution.py:257
  996.0 7.6 fusion.137
  1003.6 11.0 multiply_reduce_fusion.5
  1014.7 10.5 multiply_convert_fusion.4
  1047.7 7.5 constant_dynamic-update-slice_fusion.26
  1055.2 5.7 constant_dynamic-update-slice_fusion.27
  1075.7 7.6 fusion.137
  1083.3 11.0 multiply_reduce_fusion.5
  1094.4 10.5 multiply_convert_fusion.4
  1127.4 7.5 constant_dynamic-update-slice_fusion.26
  1134.9 5.7 constant_dynamic-update-slice_fusion.27
  1155.4 7.6 fusion.137
  1163.0 11.0 multiply_reduce_fusion.5
  1174.1 10.5 multiply_convert_fusion.4
  1207.2 7.5 constant_dynamic-update-slice_fusion.26
  1214.7 5.7 constant_dynamic-update-slice_fusion.27
  1235.1 7.6 fusion.137
  1242.8 11.0 multiply_reduce_fusion.5
  1253.8 10.5 multiply_convert_fusion.4
  1286.9 7.5 constant_dynamic-update-slice_fusion.26
  1294.4 5.7 constant_dynamic-update-slice_fusion.27
  1314.9 7.6 fusion.137
  1322.5 11.0 multiply_reduce_fusion.5
  1333.6 10.5 multiply_convert_fusion.4
  1366.7 7.4 constant_dynamic-update-slice_fusion.26
  1374.1 5.7 constant_dynamic-update-slice_fusion.27
  1394.6 7.6 fusion.137
  1402.2 11.0 multiply_reduce_fusion.5
  1413.3 10.5 multiply_convert_fusion.4
  1446.4 7.5 constant_dynamic-update-slice_fusion.26
  1453.9 5.7 constant_dynamic-update-slice_fusion.27
  1459.5 67.7 %copy.55 = f32[1312,8,1536]{2,1,0:T(8,128)} copy(f32[1312,8,1536]{0,2,1:T(8,128)} %get-tuple-element.368) | data formatting | bytes 128974848 | tf_op jit(solution)/shard_map/while | solution.py:257
  1527.3 5.2 fusion.41
  1532.7 13.0 convolution_convert_fusion.2
  1546.3 15.1 convolution_convert_fusion.1
  1565.8 334.8 %reduce-scatter.9.cloned.1.call-done = f32[164,8,1536]{2,1,0:T(8,128)} async-done(((f32[1312,8,1536]{2,1,0:T(8,128)}), f32[164,8,1536]{2,1,0:T(8,128)}) %reduce-scatter.9.cloned.1.call-update) | async-done | bytes 8060944 | tf_op jit(solution)/shard_map/reduce_scatter | solution.py:263
  1906.6 8.9 convolution_convert_fusion
  1923.4 11.5 fusion.40
  1937.3 11.0 fusion.69
  1949.3 5.6 fusion.21
  1954.9 27.6 %all-reduce.7 = (bf16[768]{0:T(1024)(128)(2,1)}, bf16[768]{0:T(1024)(128)(2,1)}, bf16[768]{0:T(1024)(128)(2,1)}, bf16[768]{0:T(1024)(128)(2,1)}, bf16[3072]{0:T(...) all-reduce(bf16[768]{0:T(1024)(128)(2,1)} %get-tuple-element.425, ...), channel_id=4, replica_groups=mesh['dp'=4,'freq'=2,'tm'=4] {'freq','tm'}, use_global_device_ids=true, to_apply=%region_22.23.clone | all-reduce | flops 7680 | bytes 30720
  1983.8 15.7 reduce-scatter.17.cloned.1.call-done
  1999.5 57.2 %reduce-scatter.15.cloned.1.call-done = bf16[96,3072]{1,0:T(8,128)(2,1)} async-done(((bf16[768,3072]{1,0:T(8,128)(2,1)}), bf16[96,3072]{1,0:T(8,128)(2,1)}) %reduce-scatter.15.cloned.1.call-update) | async-done | bytes 589840 | tf_op jit(solution)/shard_map/reduce_scatter | solution.py:299
  2056.7 51.9 %reduce-scatter.11.cloned.1.call-done = bf16[96,2304]{1,0:T(8,128)(2,1)} async-done(((bf16[768,2304]{1,0:T(8,128)(2,1)}), bf16[96,2304]{1,0:T(8,128)(2,1)}) %reduce-scatter.11.cloned.1.call-update) | async-done | bytes 442384 | tf_op jit(solution)/shard_map/reduce_scatter | solution.py:281
  2116.9 6.7 fusion.34
  2123.6 22.2 reduce-scatter.19.cloned.1.call-done
  2146.6 12.7 all-reduce.8
  2164.2 60.9 %all-reduce.12.cloned.1.call-done = (bf16[96,2304]{1,0:T(8,128)(2,1)}, bf16[96,768]{1,0:T(8,128)(2,1)}, bf16[96,3072]{1,0:T(8,128)(2,1)}, bf16[384,768]{1,0:T(8,128)(2,1)}) async-done(((bf16[96,2304]{1,0:T(8,128)(2,1)}, bf16[96,768]{1,0:T(8,128)(2,1)}, bf16[96,3072]{1,0:T(8,128)(2,1)}, bf16[384,768]{1,0:T(8,128)(2,1)}), (bf16[96,2304]{1,0:T(8,128)(2,1)}, bf16[96,768]{1,0:T(8,128)(2,1)}, ...) | async-done | bytes 1769488 | tf_op jit(solution)/shard_map/psum | solution.py:319
  (468 shorter events, 501.7 us)
Async XLA Ops:
  7.2 12.2 copy-start
  7.2 1893.5 %reduce-scatter.9.cloned.1.call-start = ((), (), s32[]{:S(2)}) async-start(), calls=%async_computation.6 | async-start | bytes 72548352 | tf_op jit(solution)/shard_map/reduce_scatter | solution.py:263
  10.9 15.3 copy-start.30
  17.4 8.9 copy-start.39
  17.4 8.9 copy-start.34
  29.1 445.8 %copy-start.53 = (bf16[3072]{0:T(1024)(128)(2,1)S(1)}, bf16[3072]{0:T(1024)(128)(2,1)}, u32[]{:S(2)}) copy-start(bf16[3072]{0:T(1024)(128)(2,1)} %param.24) | copy-start | bytes 18436
  30.3 90.1 %collective-permute-start = (bf16[164,8,1536]{2,1,0:T(8,128)(2,1)S(1)}, bf16[164,8,1536]{2,1,0:T(8,128)(2,1)S(1)}, u32[]{:S(2)}, u32[]{:S(2)}) collective-permute-start(bf16[164,8,1536]{2,1,0:T(8,128)(2,1)S(1)} %maximum_bitcast_fusion), channel_id=1, source_target_pairs={{0,1},{1,2},{2,3},{3,4},{4,5},{5,6},{6,7},{7,0},{8,9},{9,10},{10,1... | collective-permute-start | bytes 12091400 | tf_op jit(solution)/shard_map/ppermute | solution.py:138
  122.4 89.5 %collective-permute-start.1 = (bf16[164,8,1536]{2,1,0:T(8,128)(2,1)S(1)}, bf16[164,8,1536]{2,1,0:T(8,128)(2,1)S(1)}, u32[]{:S(2)}, u32[]{:S(2)}) collective-permute-start(bf16[164,8,1536]{2,1,0:T(8,128)(2,1)S(1)} %collective-permute-done), channel_id=1, source_target_pairs={{0,1},{1,2},{2,3},{3,4},{4,5},{5,6},{6,7},{7,0},{8,9},{9,10},{10,1... | collective-permute-start | bytes 12091400 | tf_op jit(solution)/shard_map/ppermute | solution.py:138
  124.0 176.7 %collective-permute-start.4 = (bf16[164,8,1536]{2,1,0:T(8,128)(2,1)S(1)}, bf16[164,8,1536]{2,1,0:T(8,128)(2,1)S(1)}, u32[]{:S(2)}, u32[]{:S(2)}) collective-permute-start(bf16[164,8,1536]{2,1,0:T(8,128)(2,1)S(1)} %maximum_bitcast_fusion), channel_id=1, source_target_pairs={{0,7},{1,0},{2,1},{3,2},{4,3},{5,4},{6,5},{7,6},{8,15},{9,8},{10,9... | collective-permute-start | bytes 12091400 | tf_op jit(solution)/shard_map/ppermute | solution.py:140
  211.8 261.8 %copy-start.17 = (bf16[164,8,1536]{2,1,0:T(8,128)(2,1)}, bf16[164,8,1536]{2,1,0:T(8,128)(2,1)S(1)}, u32[]{:S(2)}) copy-start(bf16[164,8,1536]{2,1,0:T(8,128)(2,1)S(1)} %collective-permute-done.1) | copy-start | bytes 12091396
  211.8 172.8 %collective-permute-start.2 = (bf16[164,8,1536]{2,1,0:T(8,128)(2,1)S(1)}, bf16[164,8,1536]{2,1,0:T(8,128)(2,1)}, u32[]{:S(2)}, u32[]{:S(2)}) collective-permute-start(bf16[164,8,1536]{2,1,0:T(8,128)(2,1)S(1)} %collective-permute-done.1), channel_id=1, source_target_pairs={{0,1},{1,2},{2,3},{3,4},{4,5},{5,6},{6,7},{7,0},{8,9},{9,10},{10,1... | collective-permute-start | bytes 12091400 | tf_op jit(solution)/shard_map/ppermute | solution.py:138
  302.7 170.9 %collective-permute-start.5 = (bf16[164,8,1536]{2,1,0:T(8,128)(2,1)S(1)}, bf16[164,8,1536]{2,1,0:T(8,128)(2,1)}, u32[]{:S(2)}, u32[]{:S(2)}) collective-permute-start(bf16[164,8,1536]{2,1,0:T(8,128)(2,1)S(1)} %collective-permute-done.4), channel_id=1, source_target_pairs={{0,7},{1,0},{2,1},{3,2},{4,3},{5,4},{6,5},{7,6},{8,15},{9,8},{10,9... | collective-permute-start | bytes 12091400 | tf_op jit(solution)/shard_map/ppermute | solution.py:140
  384.7 172.7 %collective-permute-start.3 = (bf16[164,8,1536]{2,1,0:T(8,128)(2,1)}, bf16[164,8,1536]{2,1,0:T(8,128)(2,1)}, u32[]{:S(2)}, u32[]{:S(2)}) collective-permute-start(bf16[164,8,1536]{2,1,0:T(8,128)(2,1)} %collective-permute-done.2), channel_id=1, source_target_pairs={{0,1},{1,2},{2,3},{3,4},{4,5},{5,6},{6,7},{7,0},{8,9},{9,10},{10,1... | collective-permute-start | bytes 12091400 | tf_op jit(solution)/shard_map/ppermute | solution.py:138
  473.6 170.7 %collective-permute-start.6 = (bf16[164,8,1536]{2,1,0:T(8,128)(2,1)}, bf16[164,8,1536]{2,1,0:T(8,128)(2,1)}, u32[]{:S(2)}, u32[]{:S(2)}) collective-permute-start(bf16[164,8,1536]{2,1,0:T(8,128)(2,1)} %collective-permute-done.5), channel_id=1, source_target_pairs={{0,7},{1,0},{2,1},{3,2},{4,3},{5,4},{6,5},{7,6},{8,15},{9,8},{10,9... | collective-permute-start | bytes 12091400 | tf_op jit(solution)/shard_map/ppermute | solution.py:140
  867.6 46.6 %copy-start.19 = (f32[1312,768]{1,0:T(8,128)}, f32[1312,768]{1,0:T(8,128)S(1)}, u32[]{:S(2)}) copy-start(f32[1312,768]{1,0:T(8,128)S(1)} %get-tuple-element.504) | copy-start | bytes 12091396
  867.7 82.3 %copy-start.41 = (f32[1312]{0:T(1024)}, f32[1312]{0:T(1024)S(1)}, u32[]{:S(2)}) copy-start(f32[1312]{0:T(1024)S(1)} %broadcast_multiply_fusion.1) | copy-start | bytes 15748
  868.3 45.9 %copy-start.45 = (f32[1312]{0:T(1024)}, f32[1312]{0:T(1024)S(1)}, u32[]{:S(2)}) copy-start(f32[1312]{0:T(1024)S(1)} %fusion.60) | copy-start | bytes 15748
  868.9 45.3 %copy-start.32 = (f32[1312]{0:T(1024)S(1)}, f32[1312]{0:T(1024)}, u32[]{:S(2)}) copy-start(f32[1312]{0:T(1024)} %convert_element_type.232) | copy-start | bytes 15748
  935.8 14.2 copy-start.38
  935.8 14.2 copy-start.20
  935.8 14.2 copy-start.46
  935.8 14.2 copy-start.50
  959.1 21.7 copy-start.25
  995.9 18.7 copy-start.2
  996.0 7.7 copy-start.4
  996.0 7.6 copy-start.29
  1014.7 14.0 copy-start.1
  1045.5 9.7 slice-start
  1075.7 18.7 copy-start.2
  1075.7 7.7 copy-start.4
  1075.7 7.6 copy-start.29
  1094.4 14.0 copy-start.1
  1125.2 9.7 slice-start
  1127.4 7.5 slice-start.1
  1155.4 18.7 copy-start.2
  1155.4 7.7 copy-start.4
  1155.4 7.6 copy-start.29
  1174.1 14.0 copy-start.1
  1205.0 9.7 slice-start
  1235.1 18.7 copy-start.2
  1235.1 7.7 copy-start.4
  1235.1 7.6 copy-start.29
  1253.8 14.0 copy-start.1
  1284.7 9.7 slice-start
  1286.9 7.5 slice-start.1
  1314.9 18.7 copy-start.2
  1314.9 7.7 copy-start.4
  1314.9 7.6 copy-start.29
  1333.6 14.0 copy-start.1
  1364.4 9.7 slice-start
  1394.5 18.7 copy-start.2
  1394.5 7.7 copy-start.4
  1394.6 7.6 copy-start.29
  1413.2 14.0 copy-start.1
  1444.1 9.8 slice-start
  1527.3 456.5 %reduce-scatter.13.cloned.1.call-start = ((), (), s32[]{:S(2)}) async-start(), calls=%async_computation.8 | async-start | bytes 1327104 | tf_op jit(solution)/shard_map/reduce_scatter | solution.py:287
  1532.6 466.9 %reduce-scatter.17.cloned.1.call-start = ((), (), s32[]{:S(2)}) async-start(), calls=%async_computation.10 | async-start | bytes 5308416 | tf_op jit(solution)/shard_map/reduce_scatter | solution.py:305
  1545.6 511.0 %reduce-scatter.15.cloned.1.call-start = ((), (), s32[]{:S(2)}) async-start(), calls=%async_computation.9 | async-start | bytes 5308416 | tf_op jit(solution)/shard_map/reduce_scatter | solution.py:299
  1561.4 547.1 %reduce-scatter.11.cloned.1.call-start = ((), (), s32[]{:S(2)}) async-start(), calls=%async_computation.7 | async-start | bytes 3981312 | tf_op jit(solution)/shard_map/reduce_scatter | solution.py:281
  1565.8 340.7 %copy-start.31 = (f32[1312]{0:T(1024)S(1)}, f32[1312]{0:T(1024)}, u32[]{:S(2)}) copy-start(f32[1312]{0:T(1024)} %copy-done.30) | copy-start | bytes 15748
  1915.5 230.3 %reduce-scatter.19.cloned.1.call-start = ((), (), s32[]{:S(2)}) async-start(), calls=%async_computation.11 | async-start | bytes 221184
  1923.3 11.5 copy-start.23
  1937.3 11.0 copy-start.40
  1949.0 276.1 %all-reduce.12.cloned.1.call-start = ((), (), s32[]{:S(2)}) async-start(), calls=%async_computation.12 | async-start | bytes 3538944 | tf_op jit(solution)/shard_map/psum | solution.py:319
  (65 other events, 248.1 us)
Sparse Core Ops, SparseCore 0:
  1527.4 373.2 reduce-scatter.8
  1904.5 36.7 reduce-scatter.12
  1945.1 54.3 reduce-scatter.16
  2002.8 53.8 reduce-scatter.14
  2060.4 48.0 reduce-scatter.10
  2112.3 33.4 reduce-scatter.18
  2148.5 76.5 all-reduce.11
